TPU v7x, 32 devices: a whole 2x2x4 slice. The times are simulated.
32 devices in a mesh: groups: 2 (over y), rows: 4 (over x, core), cents: 4 (over z).
Axes of the slice: x: 2, y: 2, z: 4, core: 2. Of those that a mesh axis runs over, the one named last changes fastest.
Arguments:
- embedding: bfloat16 [2048, 128], P(('groups', 'rows', 'cents')), parts along dimension 0, may hold values from -8 to 8
- degrees: int32 [2048], P(('groups', 'rows', 'cents')), parts along dimension 0, may hold values from 1 to 63
- rotation: float32 [128, 128], replicated, may hold values from -0.5 to 0.5
- offsets: float32 [8192, 128], P(('groups', 'cents')), parts along dimension 0, may hold values from -2 to 2
- seed_ids: int32 [8192], P(('groups', 'cents')), parts along dimension 0, may hold values from 0 to 1023
Outputs:
- energy: float32 [2048], P(('groups', 'rows', 'cents')), parts along dimension 0
- centroids: float32 [8192, 128], P(('groups', 'cents')), parts along dimension 0
There are 2 independent parts, one for each index of `groups`. A program takes and returns all parts, laid end to end along the dimension named above; an argument that names none is the same for every part. Nothing has to cross between parts.
All inputs are finite; a program needn't handle non-finite values.
Results may differ from a plain program's by a relative error of at most 0.024.
Values may be sent and summed in bfloat16 or wider, within the bound.
A program may use at most 64 MiB of HBM per device.

v0:
```python
import jax
import jax.numpy as jnp
from jax import lax
from jax.sharding import PartitionSpec as P

ITERS = 2
sharpness_scale = 0.1
ridge = 0.01


def lower_factor(matrix):
    width = matrix.shape[0]
    positions = jnp.arange(width, dtype=jnp.int32)

    def column_step(index, factor):
        row_here = lax.dynamic_index_in_dim(factor, index, 0, keepdims=False)
        column = lax.dynamic_index_in_dim(matrix, index, 1, keepdims=False)
        column = column - jnp.dot(factor, row_here, precision=lax.Precision.HIGHEST)
        pivot = jnp.sqrt(lax.dynamic_index_in_dim(column, index, 0, keepdims=False))
        column = jnp.where(positions > index, column / pivot, jnp.zeros((), column.dtype))
        column = jnp.where(positions == index, pivot, column)
        return lax.dynamic_update_slice_in_dim(factor, column[:, None], index, 1)

    return lax.fori_loop(0, width, column_step, jnp.zeros(matrix.shape, matrix.dtype))


def upper_solve(factor, target):
    width = factor.shape[0]

    def row_step(count, solved):
        index = width - 1 - count
        column = lax.dynamic_index_in_dim(factor, index, 1, keepdims=False)
        pivot = lax.dynamic_index_in_dim(column, index, 0, keepdims=False)
        target_row = lax.dynamic_index_in_dim(target, index, 0, keepdims=False)
        value = (target_row - jnp.dot(column, solved, precision=lax.Precision.HIGHEST)) / pivot
        return lax.dynamic_update_slice_in_dim(solved, value[None, :], index, 0)

    return lax.fori_loop(0, width, row_step, jnp.zeros(target.shape, target.dtype))


def block_affinity_logits(rows_block, piece_entry_lengths, cent_bf, mean_point_sqlength):
    pairwise_dots = lax.dot_general(
        rows_block, cent_bf, (((1,), (1,)), ((), ())), preferred_element_type=jnp.float32
    )
    return (
        2.0 * pairwise_dots - mean_point_sqlength[None, :] - piece_entry_lengths[:, None]
    ) / sharpness_scale


def shards(embedding, degrees, rotation, offsets, seed_ids):
    local_entries = embedding.shape[0]
    width = embedding.shape[1]
    total_rows = local_entries * lax.axis_size("rows") * lax.axis_size("cents")
    partial_gram_matrix = lax.dot_general(
        embedding, embedding, (((0,), (0,)), ((), ())), preferred_element_type=jnp.float32
    )
    gram = lax.psum(partial_gram_matrix, ("rows", "cents"))
    shifted = gram / total_rows + ridge * jnp.eye(width, dtype=jnp.float32)
    cholesky_lower_factor = lower_factor(shifted)
    turned = upper_solve(cholesky_lower_factor, rotation).astype(jnp.bfloat16)
    mixed = jnp.dot(embedding, turned, preferred_element_type=jnp.float32)
    unit = (mixed * lax.rsqrt(jnp.sum(mixed * mixed, axis=1, keepdims=True) + 1e-06)).astype(
        jnp.bfloat16
    )
    gathered, degree_rows = (
        lax.all_gather(unit, "cents", axis=0, tiled=True),
        lax.all_gather(degrees.astype(jnp.bfloat16), "cents", axis=0, tiled=True),
    )
    count = gathered.shape[0]
    weights = jnp.sqrt(degree_rows.astype(jnp.float32))
    sq_norms = jnp.sum(jnp.square(gathered.astype(jnp.float32)), axis=1)
    local_ids = seed_ids - lax.axis_index("rows") * count
    block_rows = min(512, count)
    block_count = count // block_rows
    rows_blocks = gathered.reshape(block_count, block_rows, width)
    norm_blocks = sq_norms.reshape(block_count, block_rows)
    weight_blocks = weights.reshape(block_count, block_rows)
    block_starts = jnp.arange(block_count, dtype=jnp.int32) * block_rows
    row_positions = jnp.arange(block_rows, dtype=jnp.int32)

    def seed_block(carry, pack):
        selector = ((local_ids - pack[1])[:, None] == row_positions[None, :]).astype(jnp.bfloat16)
        return (carry + jnp.dot(selector, pack[0], preferred_element_type=jnp.float32), None)

    picked_sum, unused_seed = lax.scan(
        seed_block, jnp.zeros((seed_ids.shape[0], width), jnp.float32), (rows_blocks, block_starts)
    )
    picked = picked_sum.astype(jnp.bfloat16)
    centers = lax.psum(picked, "rows").astype(jnp.float32) + offsets
    energy = jnp.zeros((count,), jnp.float32)
    for step in range(ITERS):
        cent_bf = centers.astype(jnp.bfloat16)
        mean_point_sqlength = jnp.sum(centers * centers, axis=1)

        def local_stats(pack):
            logits = block_affinity_logits(pack[0], pack[1], cent_bf, mean_point_sqlength)
            peak = jnp.max(logits, axis=1)
            return (peak, jnp.sum(jnp.exp(logits - peak[:, None]), axis=1))

        peaks, totals = lax.map(local_stats, (rows_blocks, norm_blocks))
        larger = lax.pmax(peaks, "cents")
        whole = lax.psum(totals * jnp.exp(peaks - larger), "cents")

        def accumulate(carry, pack):
            logits = block_affinity_logits(pack[0], pack[1], cent_bf, mean_point_sqlength)
            probs = jnp.exp(logits - pack[2][:, None]) / pack[3][:, None]
            shares = (pack[4][:, None] * probs).astype(jnp.bfloat16)
            moved = lax.dot_general(
                shares, pack[0], (((0,), (0,)), ((), ())), preferred_element_type=jnp.float32
            )
            return (
                (carry[0] + moved, carry[1] + jnp.sum(shares.astype(jnp.float32), axis=0)),
                None,
            )

        start = (jnp.zeros(centers.shape, jnp.float32), jnp.zeros((centers.shape[0],), jnp.float32))
        (sums, masses), unused = lax.scan(
            accumulate, start, (rows_blocks, norm_blocks, larger, whole, weight_blocks)
        )
        energy = (larger + jnp.log(whole)).reshape(count)
        full_sums, full_masses = (
            lax.psum(sums.astype(jnp.bfloat16), "rows").astype(jnp.float32),
            lax.psum(masses.astype(jnp.bfloat16), "rows").astype(jnp.float32),
        )
        centers = (full_sums + centers) / (full_masses + 1.0)[:, None]
    own_energy = lax.dynamic_slice_in_dim(
        energy, lax.axis_index("cents") * local_entries, local_entries
    )
    return (own_energy, centers)


def solution(mesh):
    placed = (
        P(("groups", "rows", "cents"), None),
        P(("groups", "rows", "cents")),
        P(),
        P(("groups", "cents"), None),
        P(("groups", "cents")),
    )
    return jax.shard_map(
        shards,
        mesh=mesh,
        in_specs=placed,
        out_specs=(P(("groups", "rows", "cents")), P(("groups", "cents"), None)),
        check_vma=False,
    )
```

profile of v0, /device:TPU:0, one launch (start us, length us, event | category | flops | bytes accessed | tf_op | source)
XLA Modules:
  0.0 808.0 jit_solution(4638034713147383374)
XLA Ops:
  12.3 13.4 %all-reduce = bf16[256]{0:T(256)(128)(2,1)S(1)} all-reduce(bf16[256]{0:T(256)(128)(2,1)S(1)} %dynamic-update-slice), channel_id=1, replica_groups=mesh['groups'=2,'rows'=4,'cents'=4] {'cents'}, use_global_device_ids=true, to_apply=%add | all-reduce | flops 256 | bytes 1024
  25.7 73.5 %all-reduce.6.cloned.1.call-done = f32[128,128]{0,1:T(8,128)} async-done(((f32[128,128]{0,1:T(8,128)}), f32[128,128]{0,1:T(8,128)}) %all-reduce.6.cloned.1.call-update) | async-done | bytes 65552 | tf_op jit(solution)/shard_map/psum | solution.py:57
  100.1 257.5 %while.22 = (s32[]{:T(128)}, f32[128,128]{1,0:T(8,128)S(1)}, f32[128,128]{0,1:T(8,128)S(1)}, s32[]{:T(128)}, s32[]{:T(128)}) while((s32[]{:T(128)}, f32[128,128]{1,0:T(8,128)S(1)}, f32[128,128]{0,1:T(8,128)S(1)}, s32[]{:T(128)}, s32[]{:T(128)}) %tuple.89), condition=%wide.region_2.3_spmd.clone.clone, body=%wide.region_1.2_spmd.clone.clone.sunk | while | flops 197378 | bytes 71269 | solution.py:24
  357.6 273.3 %while.21 = (s32[]{:T(128)}, f32[128,128]{1,0:T(8,128)S(1)}, f32[128,128]{1,0:T(8,128)}, f32[128,128]{0,1:T(8,128)S(1)}, s32[]{:T(128)}, /*index=5*/s32[]{:T(128)}, s32[]{:T(128)}, s32[]{:T(128)}) while((s32[]{:T(128)}, f32[128,128]{1,0:T(8,128)S(1)}, f32[128,128]{1,0:T(8,128)}, f32[128,128]{0,1:T(8,128)S(1)}, s32[]{:T(128)}, ...), condition=%wide.region_4.5_spmd, body=%wide.region_3.4_spmd.sunk | while | flops 196871 | bytes 69295 | solution.py:38
  358.2 1.5 fusion.51
  360.4 1.5 fusion.51
  362.5 1.5 fusion.51
  364.7 1.5 fusion.51
  366.8 1.5 fusion.51
  368.9 1.5 fusion.51
  371.1 1.5 fusion.51
  373.2 1.5 fusion.51
  392.4 1.5 fusion.51
  394.6 1.5 fusion.51
  396.7 1.5 fusion.51
  398.8 1.5 fusion.51
  401.0 1.5 fusion.51
  403.1 1.5 fusion.51
  405.2 1.5 fusion.51
  407.4 1.5 fusion.51
  435.1 1.5 fusion.51
  439.4 1.5 fusion.51
  462.9 1.5 fusion.51
  473.6 1.5 fusion.51
  497.1 1.5 fusion.51
  501.3 1.5 fusion.51
  531.2 1.5 fusion.51
  535.5 1.5 fusion.51
  539.8 1.5 fusion.51
  565.4 1.5 fusion.51
  569.7 1.5 fusion.51
  573.9 1.5 fusion.51
  578.2 1.5 fusion.51
  599.6 1.5 fusion.51
  603.8 1.5 fusion.51
  608.1 1.5 fusion.51
  612.4 1.5 fusion.51
  631.3 14.2 %all_gather.6 = bf16[256,128]{1,0:T(8,128)(2,1)S(1)} all-gather(bf16[64,128]{1,0:T(8,128)(2,1)S(1)} %fusion.23), channel_id=1, replica_groups=mesh['groups'=2,'rows'=4,'cents'=4] {'cents'}, dimensions={0}, use_global_device_ids=true | all-gather | bytes 81920 | tf_op jit(solution)/shard_map/all_gather | solution.py:66
  646.8 32.5 %all-reduce.8.cloned.1.call-done = bf16[1024,128]{1,0:T(8,128)(2,1)} async-done(((bf16[1024,128]{1,0:T(8,128)(2,1)}), bf16[1024,128]{1,0:T(8,128)(2,1)}) %all-reduce.8.cloned.1.call-update) | async-done | bytes 262160 | tf_op jit(solution)/shard_map/psum | solution.py:89
  681.0 11.7 %pmax.14 = f32[1,256]{1,0:T(1,128)S(1)} all-reduce(f32[1,256]{1,0:T(1,128)S(1)} %bitcast.76), channel_id=1, replica_groups=mesh['groups'=2,'rows'=4,'cents'=4] {'cents'}, use_global_device_ids=true, to_apply=%region_10.11 | all-reduce | flops 256 | bytes 2048 | tf_op jit(solution)/shard_map/pmax | solution.py:101
  693.0 8.4 %psum.58 = f32[256]{0:T(256)S(1)} all-reduce(f32[256]{0:T(256)S(1)} %bitcast.81), channel_id=1, replica_groups=mesh['groups'=2,'rows'=4,'cents'=4] {'cents'}, use_global_device_ids=true, to_apply=%region_12.13 | all-reduce | flops 256 | bytes 2048 | tf_op jit(solution)/shard_map/psum | solution.py:102
  701.7 5.8 psum.60
  708.6 30.8 %all-reduce.10.cloned.1.call-done = bf16[1024,128]{1,0:T(8,128)(2,1)} async-done(((bf16[1024,128]{1,0:T(8,128)(2,1)}), bf16[1024,128]{1,0:T(8,128)(2,1)}) %all-reduce.10.cloned.1.call-update) | async-done | bytes 262160 | tf_op jit(solution)/shard_map/psum | solution.py:122
  741.1 11.7 %pmax.15 = f32[1,256]{1,0:T(1,128)S(1)} all-reduce(f32[1,256]{1,0:T(1,128)S(1)} %bitcast.74), channel_id=1, replica_groups=mesh['groups'=2,'rows'=4,'cents'=4] {'cents'}, use_global_device_ids=true, to_apply=%region_18.19 | all-reduce | flops 256 | bytes 2048 | tf_op jit(solution)/shard_map/pmax | solution.py:101
  753.1 8.4 %psum.61 = f32[1,256]{1,0:T(1,128)S(1)} all-reduce(f32[1,256]{1,0:T(1,128)S(1)} %exponential_multiply_fusion), channel_id=1, replica_groups=mesh['groups'=2,'rows'=4,'cents'=4] {'cents'}, use_global_device_ids=true, to_apply=%region_20.21 | all-reduce | flops 256 | bytes 2048 | tf_op jit(solution)/shard_map/psum | solution.py:102
  761.8 5.8 psum.63
  769.3 30.2 %all-reduce.12.cloned.1.call-done = bf16[1024,128]{1,0:T(8,128)(2,1)} async-done(((bf16[1024,128]{1,0:T(8,128)(2,1)}), bf16[1024,128]{1,0:T(8,128)(2,1)}) %all-reduce.12.cloned.1.call-update) | async-done | bytes 262160 | tf_op jit(solution)/shard_map/psum | solution.py:122
  799.5 1.9 add_divide_fusion
  (1042 shorter events, 399.7 us)
Async XLA Ops:
  7.2 0.7 copy-start
  7.2 92.0 %all-reduce.6.cloned.1.call-start = ((), (), s32[]{:S(2)}) async-start(), calls=%async_computation | async-start | bytes 131072 | tf_op jit(solution)/shard_map/psum | solution.py:57
  8.8 670.5 %all-reduce.8.cloned.1.call-start = ((), (), s32[]{:S(2)}) async-start(), calls=%async_computation.1 | async-start | bytes 524288 | tf_op jit(solution)/shard_map/psum | solution.py:89
  8.8 0.7 copy-start.3
  9.5 0.7 copy-start.4
  10.2 0.7 copy-start.5
  631.0 48.3 %copy-start.1 = (f32[1024,128]{1,0:T(8,128)S(1)}, f32[1024,128]{1,0:T(8,128)}, u32[]{:S(2)}) copy-start(f32[1024,128]{1,0:T(8,128)} %param.12) | copy-start | bytes 1572868
  646.6 92.7 %all-reduce.10.cloned.1.call-start = ((), (), s32[]{:S(2)}) async-start(), calls=%async_computation.2 | async-start | bytes 524288 | tf_op jit(solution)/shard_map/psum | solution.py:122
  679.3 1.2 copy-start.2
  708.6 91.0 %all-reduce.12.cloned.1.call-start = ((), (), s32[]{:S(2)}) async-start(), calls=%async_computation.3 | async-start | bytes 524288 | tf_op jit(solution)/shard_map/psum | solution.py:122
Sparse Core Ops, SparseCore 0:
  12.0 87.1 all-reduce.5
  646.8 32.4 all-reduce.7
  708.7 30.6 all-reduce.9
  768.8 30.6 all-reduce.11
where the time goes:
time: 815 us; the launch traced here: 808 us
  local copies, waits for them, and re-layouts  225 us (28%)
  matrix products  218 us (27%)
  waiting for transfers between devices  167 us (20%)
  loops' own time  96.5 us (12%)
  blocking collectives  79.4 us (10%)
  between operations  14.6 us (2%)
  other arithmetic  8.24 us (1%)
    dot_general x128, matrix products, row_step(): jnp.dot(column, solved, precision=lax.Precision.HIGHEST)  190 us
    another operation x1, loops' own time, lower_factor(): lax.fori_loop(0, width, column_step, jnp.zeros(matrix.shape, matrix.dtype))  92.7 us
    dynamic_slice x128, local copies, waits for them, and re-layouts, column_step(): pivot = jnp.sqrt(lax.dynamic_index_in_dim(column, index, 0, keepdims=False))  81.4 us
    dynamic_slice x128, local copies, waits for them, and re-layouts, row_step(): pivot = lax.dynamic_index_in_dim(column, index, 0, keepdims=False)  75.3 us
    psum x1, waiting for transfers between devices, shards(): gram = lax.psum(partial_gram_matrix, ('rows', 'cents'))  73.5 us
    psum x2, waiting for transfers between devices, shards(): lax.psum(sums.astype(jnp.bfloat16), 'rows').astype(jnp.float32)  60.9 us
    dynamic_update_slice x128, local copies, waits for them, and re-layouts, column_step(): return lax.dynamic_update_slice_in_dim(factor, column[:, None], index, 1)  45.9 us
    psum x1, waiting for transfers between devices, shards(): centers = lax.psum(picked, 'rows').astype(jnp.float32) + offsets  32.5 us
  transfers between devices with their start and end apart: 4, of which 4 were waited for; matrix products, arithmetic and copies ran while one was open for 0% of the time, Pallas kernels for 0%

commit v1 on v0

--- a/solution.py
+++ b/solution.py
@@ -54,7 +54,7 @@
     partial_gram_matrix = lax.dot_general(
         embedding, embedding, (((0,), (0,)), ((), ())), preferred_element_type=jnp.float32
     )
-    gram = lax.psum(partial_gram_matrix, ("rows", "cents"))
+    gram = jnp.sum(lax.all_gather(partial_gram_matrix, ("rows", "cents")), axis=0)
     shifted = gram / total_rows + ridge * jnp.eye(width, dtype=jnp.float32)
     cholesky_lower_factor = lower_factor(shifted)
     turned = upper_solve(cholesky_lower_factor, rotation).astype(jnp.bfloat16)

time: 815 us -> 765 us (0.939)
  waiting for transfers between devices: 167 us -> 118 us
    psum x1 -> x0, waiting for transfers between devices: 73.5 us -> none  [shards(): gram = lax.psum(partial_gram_matrix, ('rows', 'cents'))]
    all_gather x0 -> x1, waiting for transfers between devices: none -> 26.5 us  [shards(): lax.all_gather(partial_gram_matrix, ('rows', 'cents'))]
where the time goes in v1:
time: 765 us; the launch traced here: 758 us
  local copies, waits for them, and re-layouts  224 us (29%)
  matrix products  218 us (28%)
  waiting for transfers between devices  118 us (15%)
  loops' own time  96.5 us (13%)
  blocking collectives  78.3 us (10%)
  between operations  14.5 us (2%)
  other arithmetic  8.69 us (1%)
    dot_general x128, matrix products, row_step(): jnp.dot(column, solved, precision=lax.Precision.HIGHEST)  190 us
    another operation x1, loops' own time, lower_factor(): lax.fori_loop(0, width, column_step, jnp.zeros(matrix.shape, matrix.dtype))  92.7 us
    dynamic_slice x128, local copies, waits for them, and re-layouts, column_step(): pivot = jnp.sqrt(lax.dynamic_index_in_dim(column, index, 0, keepdims=False))  81.4 us
    dynamic_slice x128, local copies, waits for them, and re-layouts, row_step(): pivot = lax.dynamic_index_in_dim(column, index, 0, keepdims=False)  75.3 us
    psum x2, waiting for transfers between devices, shards(): lax.psum(sums.astype(jnp.bfloat16), 'rows').astype(jnp.float32)  61 us
    dynamic_update_slice x128, local copies, waits for them, and re-layouts, column_step(): return lax.dynamic_update_slice_in_dim(factor, column[:, None], index, 1)  45.9 us
    psum x1, waiting for transfers between devices, shards(): centers = lax.psum(picked, 'rows').astype(jnp.float32) + offsets  30.9 us
    all_gather x1, waiting for transfers between devices, shards(): lax.all_gather(partial_gram_matrix, ('rows', 'cents'))  26.5 us
  transfers between devices with their start and end apart: 4, of which 4 were waited for; matrix products, arithmetic and copies ran while one was open for 0% of the time, Pallas kernels for 0%

profile of v1, /device:TPU:0, one launch (start us, length us, event | category | flops | bytes accessed | tf_op | source)
XLA Modules:
  0.0 758.2 jit_solution(6091484729060852537)
XLA Ops:
  11.5 13.4 %all-reduce = bf16[256]{0:T(256)(128)(2,1)S(1)} all-reduce(bf16[256]{0:T(256)(128)(2,1)S(1)} %dynamic-update-slice), channel_id=1, replica_groups=mesh['groups'=2,'rows'=4,'cents'=4] {'cents'}, use_global_device_ids=true, to_apply=%add | all-reduce | flops 256 | bytes 1024
  25.0 26.5 %all-gather.3.cloned.1.call-done = f32[2048,128]{1,0:T(8,128)} async-done(((f32[128,128]{1,0:T(8,128)}), f32[2048,128]{1,0:T(8,128)}) %all-gather.3.cloned.1.call-update) | async-done | bytes 1048592 | tf_op jit(solution)/shard_map/all_gather | solution.py:57
  52.9 257.5 %while.22 = (s32[]{:T(128)}, f32[128,128]{1,0:T(8,128)S(1)}, f32[128,128]{0,1:T(8,128)S(1)}, s32[]{:T(128)}, s32[]{:T(128)}) while((s32[]{:T(128)}, f32[128,128]{1,0:T(8,128)S(1)}, f32[128,128]{0,1:T(8,128)S(1)}, s32[]{:T(128)}, s32[]{:T(128)}) %tuple.91), condition=%wide.region_2.3_spmd.clone.clone, body=%wide.region_1.2_spmd.clone.clone.sunk | while | flops 197378 | bytes 71269 | solution.py:24
  310.5 273.3 %while.21 = (s32[]{:T(128)}, f32[128,128]{1,0:T(8,128)S(1)}, f32[128,128]{1,0:T(8,128)}, f32[128,128]{0,1:T(8,128)S(1)}, s32[]{:T(128)}, /*index=5*/s32[]{:T(128)}, s32[]{:T(128)}, s32[]{:T(128)}) while((s32[]{:T(128)}, f32[128,128]{1,0:T(8,128)S(1)}, f32[128,128]{1,0:T(8,128)}, f32[128,128]{0,1:T(8,128)S(1)}, s32[]{:T(128)}, ...), condition=%wide.region_4.5_spmd, body=%wide.region_3.4_spmd.sunk | while | flops 196871 | bytes 69295 | solution.py:38
  311.1 1.5 fusion.51
  313.2 1.5 fusion.51
  315.4 1.5 fusion.51
  317.5 1.5 fusion.51
  319.6 1.5 fusion.51
  321.8 1.5 fusion.51
  323.9 1.5 fusion.51
  347.4 1.5 fusion.51
  351.7 1.5 fusion.51
  355.9 1.5 fusion.51
  360.2 1.5 fusion.51
  381.6 1.5 fusion.51
  385.8 1.5 fusion.51
  390.1 1.5 fusion.51
  394.4 1.5 fusion.51
  415.7 1.5 fusion.51
  420.0 1.5 fusion.51
  424.3 1.5 fusion.51
  428.5 1.5 fusion.51
  449.9 1.5 fusion.51
  454.2 1.5 fusion.51
  458.4 1.5 fusion.51
  462.7 1.5 fusion.51
  484.1 1.5 fusion.51
  488.3 1.5 fusion.51
  492.6 1.5 fusion.51
  496.9 1.5 fusion.51
  522.5 1.5 fusion.51
  526.8 1.5 fusion.51
  531.0 1.5 fusion.51
  550.3 1.5 fusion.51
  560.9 1.5 fusion.51
  565.2 1.5 fusion.51
  584.2 13.1 %all_gather.14 = bf16[256,128]{1,0:T(8,128)(2,1)S(1)} all-gather(bf16[64,128]{1,0:T(8,128)(2,1)S(1)} %fusion.23), channel_id=1, replica_groups=mesh['groups'=2,'rows'=4,'cents'=4] {'cents'}, dimensions={0}, use_global_device_ids=true | all-gather | bytes 81920 | tf_op jit(solution)/shard_map/all_gather | solution.py:66
  598.6 30.9 %all-reduce.5.cloned.1.call-done = bf16[1024,128]{1,0:T(8,128)(2,1)} async-done(((bf16[1024,128]{1,0:T(8,128)(2,1)}), bf16[1024,128]{1,0:T(8,128)(2,1)}) %all-reduce.5.cloned.1.call-update) | async-done | bytes 262160 | tf_op jit(solution)/shard_map/psum | solution.py:89
  631.1 11.7 %pmax.14 = f32[1,256]{1,0:T(1,128)S(1)} all-reduce(f32[1,256]{1,0:T(1,128)S(1)} %bitcast.78), channel_id=1, replica_groups=mesh['groups'=2,'rows'=4,'cents'=4] {'cents'}, use_global_device_ids=true, to_apply=%region_10.11 | all-reduce | flops 256 | bytes 2048 | tf_op jit(solution)/shard_map/pmax | solution.py:101
  643.1 8.4 %psum.50 = f32[256]{0:T(256)S(1)} all-reduce(f32[256]{0:T(256)S(1)} %bitcast.83), channel_id=1, replica_groups=mesh['groups'=2,'rows'=4,'cents'=4] {'cents'}, use_global_device_ids=true, to_apply=%region_12.13 | all-reduce | flops 256 | bytes 2048 | tf_op jit(solution)/shard_map/psum | solution.py:102
  651.8 5.8 psum.52
  658.8 30.7 %all-reduce.7.cloned.1.call-done = bf16[1024,128]{1,0:T(8,128)(2,1)} async-done(((bf16[1024,128]{1,0:T(8,128)(2,1)}), bf16[1024,128]{1,0:T(8,128)(2,1)}) %all-reduce.7.cloned.1.call-update) | async-done | bytes 262160 | tf_op jit(solution)/shard_map/psum | solution.py:122
  691.3 11.7 %pmax.15 = f32[1,256]{1,0:T(1,128)S(1)} all-reduce(f32[1,256]{1,0:T(1,128)S(1)} %bitcast.76), channel_id=1, replica_groups=mesh['groups'=2,'rows'=4,'cents'=4] {'cents'}, use_global_device_ids=true, to_apply=%region_18.19 | all-reduce | flops 256 | bytes 2048 | tf_op jit(solution)/shard_map/pmax | solution.py:101
  703.3 8.4 %psum.53 = f32[1,256]{1,0:T(1,128)S(1)} all-reduce(f32[1,256]{1,0:T(1,128)S(1)} %exponential_multiply_fusion), channel_id=1, replica_groups=mesh['groups'=2,'rows'=4,'cents'=4] {'cents'}, use_global_device_ids=true, to_apply=%region_20.21 | all-reduce | flops 256 | bytes 2048 | tf_op jit(solution)/shard_map/psum | solution.py:102
  712.0 5.8 psum.55
  719.5 30.2 %all-reduce.9.cloned.1.call-done = bf16[1024,128]{1,0:T(8,128)(2,1)} async-done(((bf16[1024,128]{1,0:T(8,128)(2,1)}), bf16[1024,128]{1,0:T(8,128)(2,1)}) %all-reduce.9.cloned.1.call-update) | async-done | bytes 262160 | tf_op jit(solution)/shard_map/psum | solution.py:122
  749.7 1.9 add_divide_fusion
  (1044 shorter events, 399.5 us)
Async XLA Ops:
  7.2 0.7 copy-start
  7.2 44.3 %all-gather.3.cloned.1.call-start = ((), (), s32[]{:S(2)}) async-start(), calls=%async_computation.3 | async-start | bytes 1114112 | tf_op jit(solution)/shard_map/all_gather | solution.py:57
  8.7 620.7 %all-reduce.5.cloned.1.call-start = ((), (), s32[]{:S(2)}) async-start(), calls=%async_computation | async-start | bytes 524288 | tf_op jit(solution)/shard_map/psum | solution.py:89
  8.8 0.7 copy-start.4
  9.5 0.7 copy-start.5
  11.3 13.7 %copy-start.3 = (s32[1024]{0:T(1024)S(1)}, s32[1024]{0:T(1024)}, u32[]{:S(2)}) copy-start(s32[1024]{0:T(1024)} %param.13) | copy-start | bytes 12292
  583.8 45.6 %copy-start.1 = (f32[1024,128]{1,0:T(8,128)S(1)}, f32[1024,128]{1,0:T(8,128)}, u32[]{:S(2)}) copy-start(f32[1024,128]{1,0:T(8,128)} %param.12) | copy-start | bytes 1572868
  598.4 91.2 %all-reduce.7.cloned.1.call-start = ((), (), s32[]{:S(2)}) async-start(), calls=%async_computation.1 | async-start | bytes 524288 | tf_op jit(solution)/shard_map/psum | solution.py:122
  629.4 1.2 copy-start.2
  658.7 91.0 %all-reduce.9.cloned.1.call-start = ((), (), s32[]{:S(2)}) async-start(), calls=%async_computation.2 | async-start | bytes 524288 | tf_op jit(solution)/shard_map/psum | solution.py:122
Sparse Core Ops, SparseCore 0:
  10.8 40.6 all-gather.2
  598.5 30.8 all-reduce.4
  658.8 30.6 all-reduce.6
  719.0 30.6 all-reduce.8
